TPU v7x, 128 devices: a whole 4x4x4 slice. The times are simulated.
128 devices in a mesh: frame: 8 (over x_hi, z), pos: 16 (over y, x_lo, core).
Axes of the slice: x: 4 (x_hi: 2, x_lo: 2; x = x_hi * 2 + x_lo), y: 4, z: 4, core: 2. Of those that a mesh axis runs over, the one named last changes fastest.
Arguments:
- latents: bfloat16 [256, 1024, 256], P('frame', 'pos'), as said below
- gain_one: float32 [256], replicated, may hold values from 0.5 to 1.5
- query_one: bfloat16 [256, 256], replicated, as said below
- key_one: bfloat16 [256, 256], replicated, as said below
- value_one: bfloat16 [256, 256], replicated, may hold values from -0.375 to 0.375
- out_one: bfloat16 [256, 256], replicated, may hold values from -0.75 to 0.75
- gain_two: float32 [256], replicated, may hold values from 0.5 to 1.5
- query_two: bfloat16 [256, 256], replicated, as said below
- key_two: bfloat16 [256, 256], replicated, as said below
- value_two: bfloat16 [256, 256], replicated, may hold values from -0.375 to 0.375
- out_two: bfloat16 [256, 256], replicated, may hold values from -0.75 to 0.75
Outputs:
- decoded: bfloat16 [256, 1024, 256], P('frame', 'pos')
Inputs may be any that keep to these rules, and one draw needn't show every extreme that they name: `latents`: latent features of the video. `query_one`: A projection of the spatial block. `key_one`: A projection of the spatial block. `query_two`: A projection of the temporal block. `key_two`: A projection of the temporal block.
All inputs are finite; a program needn't handle non-finite values.
Results may differ from a plain program's by a relative error of at most 0.015.
The roundings to bfloat16 on the way count: a program that leaves them out, or rounds other values in their place, can miss the bound.
Values may be sent and summed in bfloat16 or wider, within the bound.
A program may use at most 320 MiB of HBM per device.

v0:
```python
import jax
import jax.numpy as jnp
from jax import lax
from jax.sharding import PartitionSpec as P

HEADS = 4


def broadcast(value, axis, source):
    kept = jnp.where(lax.axis_index(axis) == source, value, 0).astype(value.dtype)
    return lax.psum(kept, axis)


def normed(values, gain):
    wide = values.astype(jnp.float32)
    factor = lax.rsqrt(jnp.mean(wide * wide, axis=-1, keepdims=True) + 1e-06)
    return (wide * factor * gain).astype(jnp.bfloat16)


def project(values, weight):
    flat = values.reshape(-1, values.shape[-1])
    result = jnp.dot(flat, weight, preferred_element_type=jnp.float32).astype(jnp.bfloat16)
    return result.reshape(values.shape[:-1] + (weight.shape[1],))


def heads_of(values):
    return values.reshape(values.shape[:-1] + (HEADS, values.shape[-1] // HEADS))


def soft_step(carry, query, keys, vals, score_form, value_form):
    highest, totals, summed = carry
    scale = query.shape[-1] ** (-0.5)
    scores = jnp.einsum(score_form, query, keys, preferred_element_type=jnp.float32) * scale
    new_high = jnp.maximum(highest, jnp.max(scores, axis=-1))
    keep = jnp.exp(highest - new_high)
    weights = jnp.exp(scores - new_high[..., None])
    totals = totals * keep + jnp.sum(weights, axis=-1)
    summed = summed * keep[..., None] + jnp.einsum(
        value_form, weights.astype(jnp.bfloat16), vals, preferred_element_type=jnp.float32
    )
    return (new_high, totals, summed)


def empty_carry(lead, depth):
    return (
        jnp.full(lead, -1e30, jnp.float32),
        jnp.zeros(lead, jnp.float32),
        jnp.zeros(lead + (depth,), jnp.float32),
    )


def shards(
    latents,
    gain_one,
    query_one,
    key_one,
    value_one,
    out_one,
    gain_two,
    query_two,
    key_two,
    value_two,
    out_two,
):
    frames, places, width = latents.shape
    depth = width // HEADS
    normed_one = normed(latents, gain_one)
    q_one = heads_of(project(normed_one, query_one))
    k_one = project(normed_one, key_one)
    v_one = project(normed_one, value_one)
    first_keys, first_vals = (k_one[0], v_one[0])
    first_keys, first_vals = (broadcast(first_keys, "frame", 0), broadcast(first_vals, "frame", 0))
    first_keys, first_vals = (
        lax.all_gather(first_keys, "pos", axis=0, tiled=True),
        lax.all_gather(first_vals, "pos", axis=0, tiled=True),
    )
    carry = empty_carry((frames, HEADS, places), depth)
    carry = soft_step(
        carry, q_one, heads_of(first_keys), heads_of(first_vals), "fphd,khd->fhpk", "fhpk,khd->fhpd"
    )
    pieces = (
        lax.all_gather(k_one, "pos", axis=1, tiled=True),
        lax.all_gather(v_one, "pos", axis=1, tiled=True),
    )
    carry = soft_step(
        carry, q_one, heads_of(pieces[0]), heads_of(pieces[1]), "fphd,fkhd->fhpk", "fhpk,fkhd->fhpd"
    )
    attended_one = (
        (carry[2] / carry[1][..., None])
        .transpose(0, 2, 1, 3)
        .reshape(frames, places, width)
        .astype(jnp.bfloat16)
    )
    mixed_one = jnp.dot(
        attended_one.reshape(-1, width), out_one, preferred_element_type=jnp.float32
    ).reshape(frames, places, width)
    middle = (latents.astype(jnp.float32) + mixed_one).astype(jnp.bfloat16)
    normed_two = normed(middle, gain_two)
    q_two = heads_of(project(normed_two, query_two))
    carry_two = empty_carry((places, HEADS, frames), depth)
    k_two = project(normed_two, key_two)
    v_two = project(normed_two, value_two)
    pieces = (
        lax.all_gather(k_two, "frame", axis=0, tiled=True),
        lax.all_gather(v_two, "frame", axis=0, tiled=True),
    )
    carry_two = soft_step(
        carry_two,
        q_two,
        heads_of(pieces[0]),
        heads_of(pieces[1]),
        "fphd,kphd->phfk",
        "phfk,kphd->phfd",
    )
    attended_two = (
        (carry_two[2] / carry_two[1][..., None])
        .transpose(2, 0, 1, 3)
        .reshape(frames, places, width)
        .astype(jnp.bfloat16)
    )
    mixed_two = jnp.dot(
        attended_two.reshape(-1, width), out_two, preferred_element_type=jnp.float32
    ).reshape(frames, places, width)
    return (middle.astype(jnp.float32) + mixed_two).astype(jnp.bfloat16)


def solution(mesh):
    return jax.shard_map(
        shards,
        mesh=mesh,
        in_specs=(P("frame", "pos", None), P(), P(), P(), P(), P(), P(), P(), P(), P(), P()),
        out_specs=P("frame", "pos", None),
        check_vma=False,
    )
```

profile of v0, /device:TPU:1, one launch (start us, length us, event | category | flops | bytes accessed | tf_op | source)
XLA Modules:
  0.0 649.6 jit_solution(16036912624553404310)
XLA Ops:
  7.4 1.6 fusion.27
  9.0 1.6 fusion.29
  10.6 1.3 convolution_convert_fusion.3
  11.9 1.3 convolution_convert_fusion.5
  13.3 0.7 slice_select_fusion
  14.0 0.2 copy-done.3
  14.3 0.3 all-gather.5.cloned.1.call-update
  14.6 1.6 copy.78
  16.3 0.4 convolution_convert_fusion.4
  16.7 0.9 reshape_reshape.6
  17.6 1.9 copy.71
  19.5 174.5 %all-reduce.3.cloned.1.call-done = (bf16[64,256]{1,0:T(8,128)(2,1)}, bf16[64,256]{1,0:T(8,128)(2,1)}) async-done(((bf16[64,256]{1,0:T(8,128)(2,1)}, bf16[64,256]{1,0:T(8,128)(2,1)}), (bf16[64,256]{1,0:T(8,128)(2,1)}, bf16[64,256]{1,0:T(8,128)(2,1)})) %all-reduce.3.cloned.1.call-update) | async-done | bytes 65552 | tf_op jit(solution)/shard_map/psum | solution.py:11
  194.0 30.8 %all_gather.18 = bf16[1024,256]{1,0:T(8,128)(2,1)S(1)} all-gather(bf16[64,256]{1,0:T(8,128)(2,1)} %get-tuple-element.6), channel_id=1, replica_groups=mesh['frame'=8,'pos'=16] {'pos'}, dimensions={0}, use_global_device_ids=true | all-gather | bytes 557056 | tf_op jit(solution)/shard_map/all_gather | solution.py:74
  224.8 0.2 copy.70
  225.0 20.4 %all_gather.19 = bf16[1024,256]{1,0:T(8,128)(2,1)} all-gather(bf16[64,256]{1,0:T(8,128)(2,1)} %get-tuple-element.5), channel_id=1, replica_groups=mesh['frame'=8,'pos'=16] {'pos'}, dimensions={0}, use_global_device_ids=true | all-gather | bytes 557056 | tf_op jit(solution)/shard_map/all_gather | solution.py:75
  245.4 1.2 copy.72
  246.6 14.7 %fusion.50 = f32[4,1024,2048]{1,2,0} fusion(bf16[4,64,2048]{1,2,0:T(8,128)(2,1)} %bitcast.115, bf16[1024,4,64]{0,2,1:T(8,128)(2,1)S(1)} %bitcast.122), kind=kOutput, calls=%fused_computation.75 | convolution fusion | flops 1073741824 | bytes 35127296
  261.3 12.1 %bitcast_reduce_fusion = f32[32,4,64]{2,0,1:T(8,128)S(1)} fusion(f32[4,1024,32,64]{1,3,2,0:T(8,128)} %bitcast.103), kind=kLoop, calls=%fused_computation.1 | loop fusion | flops 16769024 | bytes 33587200 | tf_op jit(solution)/shard_map/reduce_max | solution.py:34
  273.5 22.5 %copy.73 = bf16[32,1024,256]{1,2,0:T(8,128)(2,1)} copy(bf16[32,1024,256]{2,1,0:T(8,128)(2,1)} %all-gather.5.cloned.1.call-done) | data formatting | bytes 33554432 | tf_op jit(solution)/shard_map/all_gather | solution.py:82
  296.1 16.5 %multiply_reduce_fusion = (f32[32,4,64]{2,1,0:T(4,128)S(1)}, f32[32,4,64,1024]{3,2,1,0:T(8,128)}) fusion(bf16[32,1024,4,64]{1,3,2,0:T(8,128)(2,1)} %bitcast.106, bf16[32,64,4,64]{3,2,1,0:T(4,128)(2,1)S(1)} %reshape_reshape.6), kind=kOutput, calls=%fused_computation.4 | convolution fusion | flops 1090510848 | bytes 51412992 | tf_op jit(solution)/shard_map/fphd,fkhd->fhpk/dot_general | solution.py:33
  312.6 14.8 %fusion.3 = f32[32,4,64]{2,0,1:T(8,128)S(1)} fusion(f32[4,1024,32,64]{1,3,2,0:T(8,128)} %bitcast.104, f32[32,4,64]{2,0,1:T(8,128)S(1)} %get-tuple-element.15), kind=kLoop, calls=%fused_computation.7 | loop fusion | flops 25157632 | bytes 33619968 | tf_op jit(solution)/shard_map/reduce_sum | solution.py:37
  327.4 5.3 copy-done.1
  332.7 9.8 %fusion.1 = (f32[32,4,64]{2,1,0:T(4,128)S(1)}, bf16[32,4,64,1024]{3,2,1,0:T(8,128)(2,1)}) fusion(f32[32,4,64,1024]{3,2,1,0:T(8,128)S(1)} %copy-done.1, f32[32,4,64]{2,1,0:T(4,128)S(1)} %copy.77), kind=kLoop, calls=%fused_computation.5 | loop fusion | flops 33546240 | bytes 50397184 | tf_op jit(solution)/shard_map/reduce_sum | solution.py:37
  342.6 16.1 %fusion.5 = f32[4,64,32,64]{3,1,2,0:T(8,128)} fusion(bf16[1024,4,64,1]{0,2,3,1:T(8,128)(2,1)S(1)} %bitcast.121, f32[4,1024,32,64]{1,3,2,0:T(8,128)} %bitcast.105, f32[32,4,64]{2,0,1:T(8,128)S(1)} %get-tuple-element.15), kind=kOutput, calls=%fused_computation.9 | convolution fusion | flops 1098907648 | bytes 36208640 | tf_op jit(solution)/shard_map/fhpk,khd->fhpd/dot_general | solution.py:38
  358.7 23.2 %copy.79 = bf16[32,1024,256]{1,2,0:T(8,128)(2,1)} copy(bf16[32,1024,256]{2,0,1:T(8,128)(2,1)} %all-gather.7.cloned.1.call-done) | data formatting | bytes 33554432 | tf_op jit(solution)/shard_map/all_gather | solution.py:83
  382.0 15.0 %fusion.19 = bf16[32,64,4,64]{1,3,0,2:T(8,128)(2,1)} fusion(f32[4,64,32,64]{3,1,2,0:T(8,128)} %fusion.5, bf16[32,1024,4,64]{1,3,2,0:T(8,128)(2,1)} %bitcast.108, bf16[32,4,64,1024]{3,2,1,0:T(8,128)(2,1)} %get-tuple-element.10, f32[32,64,4]{1,0,2:T(8,128)S(1)} %get-tuple-element.7, f32[32,64,4]{1,0,2:T(8,128)S(1)} %get-tuple-element.8, ...), kind=kOutput, calls=%fused_computation.25 | convolution fusion | flops 1076363264 | bytes 36798464 | tf_op jit(solution)/shard_map/fhpk,fkhd->fhpd/dot_general | solution.py:38
  397.0 3.1 copy.84
  400.1 2.2 convert_element_type.74
  402.3 1.8 fusion.31
  404.1 0.9 copy-done.4
  405.1 0.3 fusion.33
  405.4 1.4 convolution_convert_fusion.1
  406.9 1.5 convolution_convert_fusion
  408.5 0.4 convolution_convert_fusion.2
  408.9 0.9 reshape_reshape.7
  409.8 99.1 %all-gather.9.cloned.1.call-done = bf16[256,64,256]{2,1,0:T(8,128)(2,1)} async-done(((bf16[32,64,256]{2,1,0:T(8,128)(2,1)}), bf16[256,64,256]{2,1,0:T(8,128)(2,1)}) %all-gather.9.cloned.1.call-update) | async-done | bytes 8388624 | tf_op jit(solution)/shard_map/all_gather | solution.py:104
  508.8 13.0 %copy.85 = bf16[256,64,256]{0,2,1:T(8,128)(2,1)} copy(bf16[256,64,256]{2,1,0:T(8,128)(2,1)} %all-gather.9.cloned.1.call-done) | data formatting | bytes 16777216 | tf_op jit(solution)/shard_map/all_gather | solution.py:104
  521.8 5.7 multiply_reduce_fusion.1
  527.5 0.1 multiply_bitcast_fusion
  527.6 3.1 copy-done.2
  530.7 2.8 fusion.12
  533.6 0.1 bitcast_add_fusion.3
  533.6 82.9 %all-gather.11.cloned.1.call-done = bf16[256,64,256]{2,1,0:T(8,128)(2,1)} async-done(((bf16[32,64,256]{2,1,0:T(8,128)(2,1)}), bf16[256,64,256]{2,1,0:T(8,128)(2,1)}) %all-gather.11.cloned.1.call-update) | async-done | bytes 8388624 | tf_op jit(solution)/shard_map/all_gather | solution.py:105
  616.5 12.9 %copy.87 = bf16[256,64,256]{0,2,1:T(8,128)(2,1)} copy(bf16[256,64,256]{2,1,0:T(8,128)(2,1)} %all-gather.11.cloned.1.call-done) | data formatting | bytes 16777216 | tf_op jit(solution)/shard_map/all_gather | solution.py:105
  629.4 8.0 %fusion.17 = bf16[32,64,4,64]{3,0,2,1:T(8,128)(2,1)S(1)} fusion(f32[32,64,4]{0,2,1:T(4,128)S(1)} %bitcast_add_fusion.3, f32[32,64,4]{0,2,1:T(4,128)S(1)} %get-tuple-element.11, bf16[256,64,4,64]{0,3,2,1:T(8,128)(2,1)} %bitcast.116, f32[64,4,32,256]{3,2,1,0:T(8,128)} %copy-done.2, f32[64,4,32]{2,1,0:T(4,128)S(1)} %get-tuple-element.12), kind=kOutput, calls=%fused_computation.22 | convolution fusion | flops 276299776 | bytes 17924096 | tf_op jit(solution)/shard_map/phfk,kphd->phfd/dot_general | solution.py:38
  637.4 1.1 copy.88
  638.5 1.4 convert_element_type.83
  639.9 2.6 fusion.34
  (36 shorter events, 0.4 us)
Async XLA Ops:
  7.4 394.9 %copy-start = (bf16[256,256]{1,0:T(8,128)(2,1)S(1)}, bf16[256,256]{1,0:T(8,128)(2,1)}, u32[]{:S(2)}) copy-start(bf16[256,256]{1,0:T(8,128)(2,1)} %param.16) | copy-start | bytes 393220
  7.4 8.9 %copy-start.6 = (bf16[256,256]{1,0:T(8,128)(2,1)S(1)}, bf16[256,256]{1,0:T(8,128)(2,1)}, u32[]{:S(2)}) copy-start(bf16[256,256]{1,0:T(8,128)(2,1)} %param.13) | copy-start | bytes 393220
  7.4 186.6 %all-reduce.3.cloned.1.call-start = ((), (), s32[]{:S(2)}) async-start(), calls=%async_computation.4 | async-start | bytes 131072 | tf_op jit(solution)/shard_map/psum | solution.py:11
  13.3 1.0 copy-start.3
  14.0 259.5 %all-gather.5.cloned.1.call-start = ((), (), s32[]{:S(2)}) async-start(), calls=%async_computation | async-start | bytes 17825792 | tf_op jit(solution)/shard_map/all_gather | solution.py:82
  14.6 344.1 %all-gather.7.cloned.1.call-start = ((), (), s32[]{:S(2)}) async-start(), calls=%async_computation.1 | async-start | bytes 17825792 | tf_op jit(solution)/shard_map/all_gather | solution.py:83
  16.2 492.6 %all-gather.9.cloned.1.call-start = ((), (), s32[]{:S(2)}) async-start(), calls=%async_computation.2 | async-start | bytes 9437184 | tf_op jit(solution)/shard_map/all_gather | solution.py:104
  312.6 20.2 %copy-start.1 = (f32[32,4,64,1024]{3,2,1,0:T(8,128)S(1)}, f32[32,4,64,1024]{3,2,1,0:T(8,128)}, u32[]{:S(2)}) copy-start(f32[32,4,64,1024]{3,2,1,0:T(8,128)} %get-tuple-element.17) | copy-start | bytes 100663296
  382.0 20.3 %copy-start.5 = (bf16[32,64,256]{2,1,0:T(8,128)(2,1)S(1)}, bf16[32,64,256]{2,1,0:T(8,128)(2,1)}, u32[]{:S(2)}) copy-start(bf16[32,64,256]{2,1,0:T(8,128)(2,1)} %param.11) | copy-start | bytes 3145732
  397.0 8.1 %copy-start.11 = (f32[256]{0:T(256)S(1)}, f32[256]{0:T(256)}, u32[]{:S(2)}) copy-start(f32[256]{0:T(256)} %param.17) | copy-start | bytes 3076
  397.0 8.4 %copy-start.7 = (bf16[256,256]{1,0:T(8,128)(2,1)S(1)}, bf16[256,256]{1,0:T(8,128)(2,1)}, u32[]{:S(2)}) copy-start(bf16[256,256]{1,0:T(8,128)(2,1)} %param.19) | copy-start | bytes 393220
  397.0 9.9 %copy-start.8 = (bf16[256,256]{1,0:T(8,128)(2,1)S(1)}, bf16[256,256]{1,0:T(8,128)(2,1)}, u32[]{:S(2)}) copy-start(bf16[256,256]{1,0:T(8,128)(2,1)} %param.20) | copy-start | bytes 393220
  402.3 6.2 copy-start.9
  404.1 1.0 copy-start.4
  406.9 209.7 %all-gather.11.cloned.1.call-start = ((), (), s32[]{:S(2)}) async-start(), calls=%async_computation.3 | async-start | bytes 9437184 | tf_op jit(solution)/shard_map/all_gather | solution.py:105
  527.5 3.2 copy-start.2
  629.4 10.5 %copy-start.10 = (bf16[256,256]{1,0:T(8,128)(2,1)S(1)}, bf16[256,256]{1,0:T(8,128)(2,1)}, u32[]{:S(2)}) copy-start(bf16[256,256]{1,0:T(8,128)(2,1)} %param.21) | copy-start | bytes 393220
Sparse Core Ops, SparseCore 0:
  14.1 179.8 all-reduce.2
  407.0 101.8 all-gather.8
  511.5 105.0 all-gather.10
Sparse Core Ops, SparseCore 1:
  16.2 95.5 all-gather.4
  113.5 94.1 all-gather.6
where the time goes:
time: 652 us; the launch traced here: 650 us
  waiting for transfers between devices  357 us (55%)
  local copies, waits for them, and re-layouts  95.6 us (15%)
  matrix products  86.9 us (13%)
  blocking collectives  51.2 us (8%)
  other arithmetic  44 us (7%)
  between operations  14.9 us (2%)
    psum x1, waiting for transfers between devices, broadcast(): return lax.psum(kept, axis)  175 us
    all_gather x1, waiting for transfers between devices, shards(): lax.all_gather(k_two, 'frame', axis=0, tiled=True)  99.1 us
    all_gather x1, waiting for transfers between devices, shards(): lax.all_gather(v_two, 'frame', axis=0, tiled=True)  82.9 us
    dot_general x3, matrix products, soft_step(): jnp.einsum(value_form, weights.astype(jnp.bfloat16), vals, preferred_elem...  39.1 us
    all_gather x1, blocking collectives, shards(): lax.all_gather(first_keys, 'pos', axis=0, tiled=True)  30.8 us
    reduce_sum x3, other arithmetic, soft_step(): totals = totals * keep + jnp.sum(weights, axis=-1)  27.4 us
    all_gather x1, local copies, waits for them, and re-layouts, shards(): lax.all_gather(v_one, 'pos', axis=1, tiled=True)  23.2 us
    all_gather x1, local copies, waits for them, and re-layouts, shards(): lax.all_gather(k_one, 'pos', axis=1, tiled=True)  22.5 us
  transfers between devices with their start and end apart: 5, of which 3 were waited for; matrix products, arithmetic and copies ran while one was open for 21% of the time, Pallas kernels for 0%

commit v1 on v0

--- a/solution.py
+++ b/solution.py
@@ -6,9 +6,15 @@
 HEADS = 4
 
 
+def gather_and_add(x, axis):
+    terms = lax.all_gather(x, axis, axis=0, tiled=False)
+    total = terms.sum(axis=0)
+    return total
+
+
 def broadcast(value, axis, source):
     kept = jnp.where(lax.axis_index(axis) == source, value, 0).astype(value.dtype)
-    return lax.psum(kept, axis)
+    return gather_and_add(kept, axis)
 
 
 def normed(values, gain):

time: 652 us -> 557 us (0.85)
  waiting for transfers between devices: 357 us -> 186 us
  blocking collectives: 51.2 us -> 120 us
    psum x1 -> x0, waiting for transfers between devices: 175 us -> none  [broadcast(): return lax.psum(kept, axis)]
    all_gather x0 -> x2, blocking collectives: none -> 60.8 us  [gather_and_add(): terms = lax.all_gather(x, axis, axis=0, tiled=False)]
  transfers between devices with their start and end apart: 5 -> 4, of which waited for: 3 -> 2; matrix products, arithmetic and copies ran while one was open for 21% -> 26% of each run, Pallas kernels for 0% -> 0%
where the time goes in v1:
time: 557 us; the launch traced here: 555 us
  waiting for transfers between devices  186 us (33%)
  blocking collectives  120 us (22%)
  local copies, waits for them, and re-layouts  97.8 us (18%)
  matrix products  92.5 us (17%)
  other arithmetic  44.6 us (8%)
  between operations  13.4 us (2%)
    all_gather x1, waiting for transfers between devices, shards(): lax.all_gather(k_two, 'frame', axis=0, tiled=True)  104 us
    all_gather x1, waiting for transfers between devices, shards(): lax.all_gather(v_two, 'frame', axis=0, tiled=True)  82.5 us
    all_gather x2, blocking collectives, gather_and_add(): terms = lax.all_gather(x, axis, axis=0, tiled=False)  60.8 us
    dot_general x3, matrix products, soft_step(): jnp.einsum(value_form, weights.astype(jnp.bfloat16), vals, preferred_elem...  39.1 us
    all_gather x1, blocking collectives, shards(): lax.all_gather(first_keys, 'pos', axis=0, tiled=True)  32.4 us
    reduce_sum x3, other arithmetic, soft_step(): totals = totals * keep + jnp.sum(weights, axis=-1)  27.4 us
    all_gather x1, blocking collectives, shards(): lax.all_gather(first_vals, 'pos', axis=0, tiled=True)  26.7 us
    all_gather x1, local copies, waits for them, and re-layouts, shards(): lax.all_gather(v_one, 'pos', axis=1, tiled=True)  23.2 us
  transfers between devices with their start and end apart: 4, of which 2 were waited for; matrix products, arithmetic and copies ran while one was open for 26% of the time, Pallas kernels for 0%

profile of v1, /device:TPU:1, one launch (start us, length us, event | category | flops | bytes accessed | tf_op | source)
XLA Modules:
  0.0 554.7 jit_solution(148248662649094710)
XLA Ops:
  6.5 1.6 fusion.27
  8.2 1.6 fusion.29
  9.8 2.3 convolution_convert_fusion.5
  12.1 0.0 all-gather.9.cloned.1.call-start
  12.2 1.3 convolution_convert_fusion.3
  13.5 1.5 copy.74
  15.1 0.8 slice_select_fusion.1
  15.9 31.0 %all-gather = bf16[512,256]{1,0:T(8,128)(2,1)S(1)} all-gather(bf16[64,256]{1,0:T(8,128)(2,1)S(1)} %slice_select_fusion.1), channel_id=2, replica_groups=mesh['frame'=8,'pos'=16] {'frame'}, dimensions={0}, use_global_device_ids=true | all-gather | bytes 294912 | tf_op jit(solution)/shard_map/all_gather | solution.py:10
  47.0 32.4 %all_gather.27 = bf16[1024,256]{1,0:T(8,128)(2,1)S(1)} all-gather(bf16[64,256]{1,0:T(8,128)(2,1)S(1)} %reduce_sum.76), channel_id=1, replica_groups=mesh['frame'=8,'pos'=16] {'pos'}, dimensions={0}, use_global_device_ids=true | all-gather | bytes 557056 | tf_op jit(solution)/shard_map/all_gather | solution.py:80
  79.3 1.0 copy.66
  80.3 1.4 convolution_convert_fusion.4
  81.7 3.3 reshape_reshape.6
  85.1 1.9 copy.67
  87.0 29.8 %all-gather.1 = bf16[512,256]{1,0:T(8,128)(2,1)S(1)} all-gather(bf16[64,256]{1,0:T(8,128)(2,1)S(1)} %slice_select_fusion), channel_id=3, replica_groups=mesh['frame'=8,'pos'=16] {'frame'}, dimensions={0}, use_global_device_ids=true | all-gather | bytes 294912 | tf_op jit(solution)/shard_map/all_gather | solution.py:10
  116.8 26.7 %all_gather.29 = bf16[1024,256]{1,0:T(8,128)(2,1)S(1)} all-gather(bf16[64,256]{1,0:T(8,128)(2,1)S(1)} %reduce_sum.77), channel_id=1, replica_groups=mesh['frame'=8,'pos'=16] {'pos'}, dimensions={0}, use_global_device_ids=true | all-gather | bytes 557056 | tf_op jit(solution)/shard_map/all_gather | solution.py:81
  143.5 0.2 copy.68
  143.7 18.1 %fusion.50 = f32[4,1024,2048]{1,2,0} fusion(bf16[4,64,2048]{1,2,0:T(8,128)(2,1)} %bitcast.117, bf16[1024,4,64]{0,2,1:T(8,128)(2,1)} %bitcast.124), kind=kOutput, calls=%fused_computation.75 | convolution fusion | flops 1073741824 | bytes 35127296
  161.7 12.6 %bitcast_reduce_fusion = f32[32,4,64]{2,0,1:T(8,128)S(1)} fusion(f32[4,1024,32,64]{1,3,2,0:T(8,128)} %bitcast.105), kind=kLoop, calls=%fused_computation.1 | loop fusion | flops 16769024 | bytes 33587200 | tf_op jit(solution)/shard_map/reduce_max | solution.py:40
  174.3 22.7 %copy.69 = bf16[32,1024,256]{1,2,0:T(8,128)(2,1)} copy(bf16[32,1024,256]{2,1,0:T(8,128)(2,1)} %all-gather.7.cloned.1.call-done) | data formatting | bytes 33554432 | tf_op jit(solution)/shard_map/all_gather | solution.py:88
  197.0 16.8 %multiply_reduce_fusion = (f32[32,4,64]{2,1,0:T(4,128)S(1)}, f32[32,4,64,1024]{3,2,1,0:T(8,128)}) fusion(bf16[32,1024,4,64]{1,3,2,0:T(8,128)(2,1)} %bitcast.108, bf16[32,64,4,64]{3,2,1,0:T(4,128)(2,1)S(1)} %reshape_reshape.6), kind=kOutput, calls=%fused_computation.4 | convolution fusion | flops 1090510848 | bytes 51412992 | tf_op jit(solution)/shard_map/fphd,fkhd->fhpk/dot_general | solution.py:39
  213.9 14.8 %fusion.3 = f32[32,4,64]{2,0,1:T(8,128)S(1)} fusion(f32[4,1024,32,64]{1,3,2,0:T(8,128)} %bitcast.106, f32[32,4,64]{2,0,1:T(8,128)S(1)} %get-tuple-element.13), kind=kLoop, calls=%fused_computation.7 | loop fusion | flops 25157632 | bytes 33619968 | tf_op jit(solution)/shard_map/reduce_sum | solution.py:43
  228.8 5.3 copy-done.1
  234.1 9.8 %fusion.1 = (f32[32,4,64]{2,1,0:T(4,128)S(1)}, bf16[32,4,64,1024]{3,2,1,0:T(8,128)(2,1)}) fusion(f32[32,4,64,1024]{3,2,1,0:T(8,128)S(1)} %copy-done.1, f32[32,4,64]{2,1,0:T(4,128)S(1)} %copy.73), kind=kLoop, calls=%fused_computation.5 | loop fusion | flops 33546240 | bytes 50397184 | tf_op jit(solution)/shard_map/reduce_sum | solution.py:43
  243.9 16.1 %fusion.5 = f32[4,64,32,64]{3,1,2,0:T(8,128)} fusion(bf16[1024,4,64,1]{0,2,3,1:T(8,128)(2,1)S(1)} %bitcast.123, f32[4,1024,32,64]{1,3,2,0:T(8,128)} %bitcast.107, f32[32,4,64]{2,0,1:T(8,128)S(1)} %get-tuple-element.13), kind=kOutput, calls=%fused_computation.9 | convolution fusion | flops 1098907648 | bytes 36208640 | tf_op jit(solution)/shard_map/fhpk,khd->fhpd/dot_general | solution.py:44
  260.0 23.2 %copy.75 = bf16[32,1024,256]{1,2,0:T(8,128)(2,1)} copy(bf16[32,1024,256]{2,0,1:T(8,128)(2,1)} %all-gather.9.cloned.1.call-done) | data formatting | bytes 33554432 | tf_op jit(solution)/shard_map/all_gather | solution.py:89
  283.2 15.0 %fusion.19 = bf16[32,64,4,64]{1,3,0,2:T(8,128)(2,1)} fusion(f32[4,64,32,64]{3,1,2,0:T(8,128)} %fusion.5, bf16[32,1024,4,64]{1,3,2,0:T(8,128)(2,1)} %bitcast.110, bf16[32,4,64,1024]{3,2,1,0:T(8,128)(2,1)} %get-tuple-element.8, f32[32,64,4]{1,0,2:T(8,128)S(1)} %get-tuple-element.5, f32[32,64,4]{1,0,2:T(8,128)S(1)} %get-tuple-element.6, ...), kind=kOutput, calls=%fused_computation.25 | convolution fusion | flops 1076363264 | bytes 36798464 | tf_op jit(solution)/shard_map/fhpk,fkhd->fhpd/dot_general | solution.py:44
  298.3 3.1 copy.80
  301.4 2.2 convert_element_type.78
  303.6 1.8 fusion.31
  305.4 0.9 copy-done.3
  306.3 0.3 fusion.33
  306.7 1.4 convolution_convert_fusion.1
  308.2 1.5 convolution_convert_fusion
  309.7 0.4 convolution_convert_fusion.2
  310.2 0.9 reshape_reshape.7
  311.0 103.9 %all-gather.11.cloned.1.call-done = bf16[256,64,256]{2,1,0:T(8,128)(2,1)} async-done(((bf16[32,64,256]{2,1,0:T(8,128)(2,1)}), bf16[256,64,256]{2,1,0:T(8,128)(2,1)}) %all-gather.11.cloned.1.call-update) | async-done | bytes 8388624 | tf_op jit(solution)/shard_map/all_gather | solution.py:110
  414.9 13.0 %copy.81 = bf16[256,64,256]{0,2,1:T(8,128)(2,1)} copy(bf16[256,64,256]{2,1,0:T(8,128)(2,1)} %all-gather.11.cloned.1.call-done) | data formatting | bytes 16777216 | tf_op jit(solution)/shard_map/all_gather | solution.py:110
  427.9 5.6 %multiply_reduce_fusion.1 = (f32[64,4,32]{2,1,0:T(4,128)S(1)}, f32[64,4,32,256]{3,2,1,0:T(8,128)S(1)}) fusion(bf16[256,64,4,64]{0,3,2,1:T(8,128)(2,1)} %bitcast.109, bf16[32,64,4,64]{3,2,1,0:T(4,128)(2,1)S(1)} %reshape_reshape.7), kind=kOutput, calls=%fused_computation.16 | convolution fusion | flops 272621568 | bytes 17858560 | tf_op jit(solution)/shard_map/fphd,kphd->phfk/dot_general | solution.py:39
  433.5 0.1 multiply_bitcast_fusion
  433.6 3.1 copy-done.2
  436.7 2.8 fusion.12
  439.6 0.1 bitcast_add_fusion.3
  439.7 82.5 %all-gather.13.cloned.1.call-done = bf16[256,64,256]{2,1,0:T(8,128)(2,1)} async-done(((bf16[32,64,256]{2,1,0:T(8,128)(2,1)}), bf16[256,64,256]{2,1,0:T(8,128)(2,1)}) %all-gather.13.cloned.1.call-update) | async-done | bytes 8388624 | tf_op jit(solution)/shard_map/all_gather | solution.py:111
  522.2 12.9 %copy.83 = bf16[256,64,256]{0,2,1:T(8,128)(2,1)} copy(bf16[256,64,256]{2,1,0:T(8,128)(2,1)} %all-gather.13.cloned.1.call-done) | data formatting | bytes 16777216 | tf_op jit(solution)/shard_map/all_gather | solution.py:111
  535.0 8.0 %fusion.17 = bf16[32,64,4,64]{3,0,2,1:T(8,128)(2,1)S(1)} fusion(f32[32,64,4]{0,2,1:T(4,128)S(1)} %bitcast_add_fusion.3, f32[32,64,4]{0,2,1:T(4,128)S(1)} %get-tuple-element.9, bf16[256,64,4,64]{0,3,2,1:T(8,128)(2,1)} %bitcast.118, f32[64,4,32,256]{3,2,1,0:T(8,128)} %copy-done.2, f32[64,4,32]{2,1,0:T(4,128)S(1)} %get-tuple-element.10), kind=kOutput, calls=%fused_computation.22 | convolution fusion | flops 276299776 | bytes 17924096 | tf_op jit(solution)/shard_map/phfk,kphd->phfd/dot_general | solution.py:44
  543.0 1.1 copy.84
  544.1 1.4 convert_element_type.87
  545.5 2.6 fusion.34
  (36 shorter events, 0.4 us)
Async XLA Ops:
  6.5 297.0 %copy-start = (bf16[256,256]{1,0:T(8,128)(2,1)S(1)}, bf16[256,256]{1,0:T(8,128)(2,1)}, u32[]{:S(2)}) copy-start(bf16[256,256]{1,0:T(8,128)(2,1)} %param.16) | copy-start | bytes 393220
  6.5 73.8 %copy-start.5 = (bf16[256,256]{1,0:T(8,128)(2,1)S(1)}, bf16[256,256]{1,0:T(8,128)(2,1)}, u32[]{:S(2)}) copy-start(bf16[256,256]{1,0:T(8,128)(2,1)} %param.13) | copy-start | bytes 393220
  6.5 167.8 %all-gather.7.cloned.1.call-start = ((), (), s32[]{:S(2)}) async-start(), calls=%async_computation | async-start | bytes 17825792 | tf_op jit(solution)/shard_map/all_gather | solution.py:88
  12.1 247.9 %all-gather.9.cloned.1.call-start = ((), (), s32[]{:S(2)}) async-start(), calls=%async_computation.1 | async-start | bytes 17825792 | tf_op jit(solution)/shard_map/all_gather | solution.py:89
  15.1 399.8 %all-gather.11.cloned.1.call-start = ((), (), s32[]{:S(2)}) async-start(), calls=%async_computation.2 | async-start | bytes 9437184 | tf_op jit(solution)/shard_map/all_gather | solution.py:110
  213.9 20.2 %copy-start.1 = (f32[32,4,64,1024]{3,2,1,0:T(8,128)S(1)}, f32[32,4,64,1024]{3,2,1,0:T(8,128)}, u32[]{:S(2)}) copy-start(f32[32,4,64,1024]{3,2,1,0:T(8,128)} %get-tuple-element.15) | copy-start | bytes 100663296
  283.2 20.3 %copy-start.4 = (bf16[32,64,256]{2,1,0:T(8,128)(2,1)S(1)}, bf16[32,64,256]{2,1,0:T(8,128)(2,1)}, u32[]{:S(2)}) copy-start(bf16[32,64,256]{2,1,0:T(8,128)(2,1)} %param.11) | copy-start | bytes 3145732
  298.3 8.1 %copy-start.10 = (f32[256]{0:T(256)S(1)}, f32[256]{0:T(256)}, u32[]{:S(2)}) copy-start(f32[256]{0:T(256)} %param.17) | copy-start | bytes 3076
  298.3 8.4 %copy-start.6 = (bf16[256,256]{1,0:T(8,128)(2,1)S(1)}, bf16[256,256]{1,0:T(8,128)(2,1)}, u32[]{:S(2)}) copy-start(bf16[256,256]{1,0:T(8,128)(2,1)} %param.19) | copy-start | bytes 393220
  298.3 9.9 %copy-start.7 = (bf16[256,256]{1,0:T(8,128)(2,1)S(1)}, bf16[256,256]{1,0:T(8,128)(2,1)}, u32[]{:S(2)}) copy-start(bf16[256,256]{1,0:T(8,128)(2,1)} %param.20) | copy-start | bytes 393220
  303.6 6.2 %copy-start.8 = (bf16[256,256]{1,0:T(8,128)(2,1)S(1)}, bf16[256,256]{1,0:T(8,128)(2,1)}, u32[]{:S(2)}) copy-start(bf16[256,256]{1,0:T(8,128)(2,1)} %param.18) | copy-start | bytes 393220
  305.4 1.0 copy-start.3
  308.2 214.0 %all-gather.13.cloned.1.call-start = ((), (), s32[]{:S(2)}) async-start(), calls=%async_computation.3 | async-start | bytes 9437184 | tf_op jit(solution)/shard_map/all_gather | solution.py:111
  433.5 3.2 copy-start.2
  535.0 10.5 %copy-start.9 = (bf16[256,256]{1,0:T(8,128)(2,1)S(1)}, bf16[256,256]{1,0:T(8,128)(2,1)}, u32[]{:S(2)}) copy-start(bf16[256,256]{1,0:T(8,128)(2,1)} %param.21) | copy-start | bytes 393220
Sparse Core Ops, SparseCore 0:
  12.2 104.1 all-gather.6
  118.1 93.8 all-gather.8
  308.3 106.5 all-gather.10
  417.1 105.0 all-gather.12
